TPU v7x, 256 devices: a whole 4x4x8 slice. The times are simulated.
256 devices in a mesh: genome: 32 (over z, x), anc: 4 (over y_lo, core), trait: 2 (over y_hi).
Axes of the slice: x: 4, y: 4 (y_hi: 2, y_lo: 2; y = y_hi * 2 + y_lo), z: 8, core: 2. Of those that a mesh axis runs over, the one named last changes fastest.
Arguments:
- coefficients: float32 [4, 128, 65536], P('anc', 'trait', 'genome'), may hold values from -3 to 3
- sumstats: float32 [4, 128, 65536], P('anc', 'trait', 'genome'), may hold values from -12 to 12
- linkage: bfloat16 [4, 65536, 4096], P('anc', 'genome'), may hold values from -0.09375 to 0.09375
- band_start: int32 [4, 256], P('anc', 'genome'), may hold values from 0 to 61440, as said below
- group_ids: int32 [4, 65536], P('anc', 'genome'), may hold values from 0 to 63, never falling along the last dimension, each value on 1 to 8192 neighbouring positions
- group_weight: float32 [4, 64], P('anc'), may hold values from 0.1 to 1.5
- dosage: bfloat16 [4, 2048, 65536], P('anc', None, 'genome'), may hold values from 0 to 2
Outputs:
- updated: float32 [4, 128, 65536], P('anc', 'trait', 'genome')
- scores: float32 [4, 128, 2048], P('anc', 'trait', 'genome')
Inputs may be any that keep to these rules, and one draw needn't show every extreme that they name: band_start[a, u] is the first of the 4096 consecutive SNP columns stored in linkage[a] for row block u, the SNPs u * 256 to u * 256 + 255; these columns always include the block's own SNPs. `group_ids`: group ids never fall along the SNPs of an ancestry, so each group is one run of consecutive SNPs.
All inputs are finite; a program needn't handle non-finite values.
Results may differ from a plain program's by a relative error of at most 0.003.
Values may be sent and summed in bfloat16 or wider, within the bound.
No kernel may reach another device: no remote copies, remote signals or barrier semaphores. Data moves between devices by JAX's collectives and lax.ppermute only.
A program may use at most 128 MiB of HBM per device.

v0:
```python
import math
import jax
import jax.numpy as jnp
from jax import lax
from jax.sharding import PartitionSpec as P

TRAITS = 128
TILE = 256
step_size = 0.5
merging = 0.5
epsilon = 1e-06


def total_of_pieces(value, axis):
    parts = lax.all_gather(value, axis)
    return parts.sum(axis=0)


def passed_along(block, axis, distance):
    devices = range(lax.axis_size(axis))
    route = [(i - distance, i) for i in devices if i - distance in devices]
    return lax.ppermute(block, axis, route)


def sent_to_all(value, axis):
    copies = jnp.broadcast_to(value, (lax.axis_size(axis), *value.shape))
    return lax.all_to_all(copies, axis, split_axis=0, concat_axis=0, tiled=True)


def over_copies(value, axis):
    return sent_to_all(value, axis).sum(axis=0)


def rows_first(arrays, axis, dims):
    turned = [jnp.moveaxis(a, dim, 0) for a, dim in zip(arrays, dims)]
    both = jnp.concatenate([t.reshape(len(t), -1) for t in turned], axis=1)
    result, at, done = (lax.all_gather(both, axis, axis=0, tiled=True), 0, [])
    for t, dim in zip(turned, dims):
        piece = result[:, at : at + t[0].size].reshape(-1, *t.shape[1:])
        done.append(jnp.moveaxis(piece, 0, dim))
        at += t[0].size
    return tuple(done)


def cut_along(value, dim, peers):
    dims = value.shape
    parts = value.reshape(*dims[:dim], peers, dims[dim] // peers, *dims[dim + 1 :])
    return jnp.moveaxis(parts, dim, 0)


def sent_and_summed(value, axis, dim):
    parts = cut_along(value, dim, lax.axis_size(axis))
    arrived = lax.all_to_all(parts, axis, split_axis=0, concat_axis=0, tiled=True)
    return arrived.sum(axis=0)


def per_device(coefficients, sumstats, linkage, band_start, group_ids, group_weight, dosage):
    current = coefficients[0]
    targets = sumstats[0]
    band = linkage[0]
    starts = band_start[0]
    group_list = group_ids[0]
    weights = group_weight[0]
    genotype = dosage[0]
    traits_here, snp_rows = current.shape
    band_width = band.shape[1]
    reach_count = band_width // snp_rows
    genome_count = lax.axis_size("genome")
    position = lax.axis_index("genome")
    anchor = position * snp_rows
    ancestries = lax.axis_size("anc") * coefficients.shape[0]
    mean_coef = total_of_pieces(current, "anc") / ancestries
    low_copy = current.astype(jnp.bfloat16)
    below_list = []
    above_list = []
    for distance in range(1, reach_count + 1):
        below_list.insert(0, passed_along(low_copy, "genome", distance))
        above_list.append(passed_along(low_copy, "genome", -distance))
    extended = jnp.concatenate(below_list + [low_copy] + above_list, axis=1)
    local_start = starts - anchor + band_width
    windows = jax.vmap(
        lambda begin_at: lax.dynamic_slice_in_dim(extended, begin_at, band_width, 1)
    )(local_start)
    band_tiles = band.reshape(snp_rows // TILE, TILE, band_width)
    products = jnp.einsum("ntw,nrw->tnr", windows, band_tiles, preferred_element_type=jnp.float32)
    band_product = products.reshape(traits_here, snp_rows)
    gradient = current + band_product - targets + merging * (current - mean_coef)
    proposal = current - step_size * gradient
    trait_part = jnp.sum(proposal * proposal, axis=0)
    trait_total = over_copies(trait_part, "trait")
    same_group = (group_list[:, None] == group_list[None, :]).astype(jnp.float32)
    local_squares = jnp.dot(same_group, trait_total, precision=lax.Precision.HIGHEST)
    local_counts = jnp.sum(same_group, axis=1)
    id_float = group_list.astype(jnp.float32)
    first_id = id_float[0]
    last_id = id_float[-1]
    edge_values = rows_first(
        (
            first_id[None],
            last_id[None],
            local_squares[:1],
            local_counts[:1],
            local_squares[-1:],
            local_counts[-1:],
        ),
        "genome",
        (0, 0, 0, 0, 0, 0),
    )
    firsts, lasts, head_squares, head_counts, tail_squares, tail_counts = edge_values
    others = (jnp.arange(genome_count, dtype=jnp.int32) != position)[None, :]
    at_head = id_float[:, None] == firsts[None, :]
    at_tail = id_float[:, None] == lasts[None, :]
    square_terms = jnp.where(
        at_head, head_squares[None, :], jnp.where(at_tail, tail_squares[None, :], 0.0)
    )
    count_terms = jnp.where(
        at_head, head_counts[None, :], jnp.where(at_tail, tail_counts[None, :], 0.0)
    )
    extra_squares = jnp.sum(jnp.where(others, square_terms, 0.0), axis=1)
    extra_counts = jnp.sum(jnp.where(others, count_terms, 0.0), axis=1)
    group_squares = local_squares + extra_squares
    group_counts = local_counts + extra_counts
    lookup = (group_list[:, None] == jnp.arange(weights.shape[0], dtype=jnp.int32)[None, :]).astype(
        jnp.float32
    )
    snp_weight = jnp.dot(lookup, weights, precision=lax.Precision.HIGHEST)
    threshold = step_size * snp_weight * jnp.sqrt(group_counts * TRAITS)
    factor = jnp.maximum(0.0, 1.0 - threshold / jnp.sqrt(group_squares + epsilon))
    updated = proposal * factor[None, :]
    snps_total = snp_rows * genome_count
    partial_value = lax.dot_general(
        updated.astype(jnp.bfloat16),
        genotype,
        (((1,), (1,)), ((), ())),
        preferred_element_type=jnp.float32,
    ) / math.sqrt(snps_total)
    scores = sent_and_summed(partial_value, "genome", 1)
    return (updated[None], scores[None])


def solution(mesh):
    in_specs = (
        P("anc", "trait", "genome"),
        P("anc", "trait", "genome"),
        P("anc", "genome", None),
        P("anc", "genome"),
        P("anc", "genome"),
        P("anc", None),
        P("anc", None, "genome"),
    )
    out_specs = (P("anc", "trait", "genome"), P("anc", "trait", "genome"))
    return jax.shard_map(
        per_device, mesh=mesh, in_specs=in_specs, out_specs=out_specs, check_vma=False
    )
```

profile of v0, /device:TPU:32, one launch (start us, length us, event | category | flops | bytes accessed | tf_op | source)
XLA Modules:
  0.0 168.4 jit_solution(14491899200398587660)
XLA Ops:
  7.2 1.1 bitcast_convert_fusion
  8.3 4.9 %collective-permute-start = (bf16[64,2048]{1,0:T(8,128)(2,1)S(1)}, bf16[64,2048]{1,0:T(8,128)(2,1)S(1)}, u32[]{:S(2)}, u32[]{:S(2)}) collective-permute-start(bf16[64,2048]{1,0:T(8,128)(2,1)S(1)} %bitcast_convert_fusion), channel_id=1, source_target_pairs={{0,16},{8,24},{16,32},{24,40},{32,48},{40,56},{48,64},{56,72},{64,... | collective-permute-start | bytes 786440 | tf_op jit(solution)/shard_map/ppermute | solution.py:22
  13.2 2.5 %collective-permute-start.1 = (bf16[64,2048]{1,0:T(8,128)(2,1)S(1)}, bf16[64,2048]{1,0:T(8,128)(2,1)S(1)}, u32[]{:S(2)}, u32[]{:S(2)}) collective-permute-start(bf16[64,2048]{1,0:T(8,128)(2,1)S(1)} %bitcast_convert_fusion), channel_id=1, source_target_pairs={{0,8},{8,16},{16,24},{24,32},{32,40},{40,48},{48,56},{56,64},{64,7... | collective-permute-start | bytes 786440 | tf_op jit(solution)/shard_map/ppermute | solution.py:22
  15.7 5.5 %collective-permute-start.2 = (bf16[64,2048]{1,0:T(8,128)(2,1)S(1)}, bf16[64,2048]{1,0:T(8,128)(2,1)S(1)}, u32[]{:S(2)}, u32[]{:S(2)}) collective-permute-start(bf16[64,2048]{1,0:T(8,128)(2,1)S(1)} %bitcast_convert_fusion), channel_id=1, source_target_pairs={{8,0},{16,8},{24,16},{32,24},{40,32},{48,40},{56,48},{64,56},{72,6... | collective-permute-start | bytes 786440 | tf_op jit(solution)/shard_map/ppermute | solution.py:22
  21.2 1.9 %collective-permute-start.3 = (bf16[64,2048]{1,0:T(8,128)(2,1)S(1)}, bf16[64,2048]{1,0:T(8,128)(2,1)S(1)}, u32[]{:S(2)}, u32[]{:S(2)}) collective-permute-start(bf16[64,2048]{1,0:T(8,128)(2,1)S(1)} %bitcast_convert_fusion), channel_id=1, source_target_pairs={{16,0},{24,8},{32,16},{40,24},{48,32},{56,40},{64,48},{72,56},{80,... | collective-permute-start | bytes 786440 | tf_op jit(solution)/shard_map/ppermute | solution.py:22
  23.2 2.5 %fusion.2 = f32[2048]{0:T(1024)S(1)} fusion(s32[2048]{0:T(1024)} %bitcast.93), kind=kLoop, calls=%fused_computation.5 | loop fusion | flops 12580864 | bytes 16384 | tf_op jit(solution)/shard_map/reduce_sum | solution.py:93
  25.7 1.4 fusion.10
  27.1 0.7 compare_select_fusion.4
  27.8 0.7 convert_element_type.22
  29.8 1.1 constant_dynamic-update-slice_fusion.2
  30.9 1.9 %collective-permute-done.3 = bf16[64,2048]{1,0:T(8,128)(2,1)S(1)} collective-permute-done((bf16[64,2048]{1,0:T(8,128)(2,1)S(1)}, bf16[64,2048]{1,0:T(8,128)(2,1)S(1)}, u32[]{:S(2)}, u32[]{:S(2)}) %collective-permute-start.3) | collective-permute-done | bytes 262176 | tf_op jit(solution)/shard_map/ppermute | solution.py:22
  32.8 18.1 %while.1 = (s32[]{:T(128)}, bf16[64,10240]{1,0:T(8,128)(2,1)S(1)}, s32[8,2]{0,1:T(2,128)S(1)}, bf16[8,64,4096]{2,1,0:T(8,128)(2,1)}, s32[]{:T(128)}) while((s32[]{:T(128)}, bf16[64,10240]{1,0:T(8,128)(2,1)S(1)}, s32[8,2]{0,1:T(2,128)S(1)}, bf16[8,64,4096]{2,1,0:T(8,128)(2,1)}, s32[]{:T(128)}) %tuple.29), condition=%wide.while_cond, body=%wide.while_body.sunk | while | flops 2 | bytes 1049689 | solution.py:82
  33.4 1.6 bitcast_dynamic-update-slice_fusion.2
  35.7 1.7 bitcast_dynamic-update-slice_fusion.2
  37.9 1.7 bitcast_dynamic-update-slice_fusion.2
  40.2 1.7 bitcast_dynamic-update-slice_fusion.2
  42.5 1.6 bitcast_dynamic-update-slice_fusion.2
  44.7 1.7 bitcast_dynamic-update-slice_fusion.2
  47.0 1.6 bitcast_dynamic-update-slice_fusion.2
  49.3 1.7 bitcast_dynamic-update-slice_fusion.2
  50.9 12.4 %fusion.33 = f32[8,64,256]{2,1,0:T(8,128)S(1)} fusion(bf16[8,64,4096]{2,1,0:T(8,128)(2,1)} %get-tuple-element.9, bf16[8,256,4096]{2,1,0:T(8,128)(2,1)} %bitcast.83), kind=kOutput, calls=%fused_computation.59 | convolution fusion | flops 1073741824 | bytes 21495808 | tf_op jit(solution)/shard_map/ntw,nrw->tnr/dot_general | solution.py:85
  63.4 1.8 %reduce_sum.63 = f32[64,2048]{1,0:T(8,128)S(1)} reduce(f32[4,64,2048]{2,1,0:T(8,128)} %all-gather.3.cloned.1.call-done, f32[]{:T(128)} %constant.8.clone.1), dimensions={0}, to_apply=%region_0.0 | reduce | flops 393216 | bytes 2621444 | tf_op jit(solution)/shard_map/reduce_sum | solution.py:16
  66.0 4.5 %all-to-all-start = ((f32[2,1,2048]{2,1,0:T(1,128)}), f32[2,1,2048]{2,1,0:T(1,128)S(1)}, u32[]{:S(2)}, u32[]{:S(2)}) async-start(f32[2,1,2048]{2,1,0:T(1,128)} %broadcast_in_dim.67), calls=%async_computation | async-start | bytes 32768 | tf_op jit(solution)/shard_map/all_to_all | solution.py:27
  70.9 5.0 %all-to-all-done = f32[2,1,2048]{2,1,0:T(1,128)S(1)} async-done(((f32[2,1,2048]{2,1,0:T(1,128)}), f32[2,1,2048]{2,1,0:T(1,128)S(1)}, u32[]{:S(2)}, u32[]{:S(2)}) %all-to-all-start) | async-done | bytes 16416 | tf_op jit(solution)/shard_map/all_to_all | solution.py:27
  75.9 6.9 %fusion = f32[1,2048]{1,0:T(1,128)S(1)} fusion(f32[2048,1]{0,1:T(1,128)S(1)} %bitcast.92, s32[2048]{0:T(1024)S(1)} %bitcast.96), kind=kOutput, calls=%fused_computation.2 | convolution fusion | flops 54525952 | bytes 24576 | tf_op jit(solution)/shard_map/dot_general | solution.py:92
  83.4 3.9 %concatenate.11 = f32[1,6]{1,0:T(1,128)S(1)} concatenate(f32[1,1]{1,0:T(1,128)} %bitcast.10, f32[1,1]{1,0:T(1,128)} %bitcast.11, f32[1,1]{1,0:T(1,128)} %bitcast.15, f32[1,1]{1,0:T(1,128)} %bitcast.16, f32[1,1]{1,0:T(1,128)} %bitcast.17, f32[1,1]{1,0:T(1,128)} %bitcast.18), dimensions={1} | concatenate | bytes 48 | tf_op jit(solution)/shard_map/concatenate | solution.py:36
  87.4 42.7 %all-gather = f32[32,1,6]{2,1,0:T(1,128)S(1)} all-gather(f32[1,1,6]{2,1,0:T(1,128)S(1)} %bitcast.98), channel_id=1, replica_groups=mesh['genome'=32,'anc'=4,'trait'=2] {'genome'}, dimensions={0}, use_global_device_ids=true | all-gather | bytes 792 | tf_op jit(solution)/shard_map/all_gather | solution.py:37
  130.8 6.2 %fusion.7 = f32[64,2048]{1,0:T(8,128)S(1)} fusion(bf16[1,2048,2048]{2,1,0:T(8,128)(2,1)} %param.13, f32[1,64,2048]{2,1,0:T(8,128)S(1)} %fusion.20), kind=kOutput, calls=%fused_computation.10 | convolution fusion | flops 537133056 | bytes 9437184 | tf_op jit(solution)/shard_map/dot_general | solution.py:131
  138.0 0.7 reshape.135
  138.7 19.3 %all_to_all.11 = f32[32,1,4096]{2,1,0:T(1,128)S(1)} all-to-all(f32[32,1,4096]{2,1,0:T(1,128)S(1)} %reshape.135), channel_id=1, replica_groups=mesh['genome'=32,'anc'=4,'trait'=2] {'genome'}, dimensions={0} | all-to-all | bytes 1048576 | tf_op jit(solution)/shard_map/all_to_all | solution.py:53
  158.5 1.9 %reduce.13 = f32[32,4096]{1,0:T(8,128)S(1)} reduce(f32[32,1,4096]{2,1,0:T(1,128)S(1)} %all_to_all.11, f32[]{:T(128)} %broadcast.110), dimensions={1}, to_apply=%all_to_all.8.reduce_sub_computation | reduce | bytes 1048580 | tf_op jit(solution)/shard_map/all_to_all | solution.py:53
  160.9 0.7 reduce_sum.69
  (56 shorter events, 10.8 us)
Async XLA Ops:
  7.2 18.5 %copy-start = (f32[1,64]{1,0:T(1,128)S(1)}, f32[1,64]{1,0:T(1,128)}, u32[]{:S(2)}) copy-start(f32[1,64]{1,0:T(1,128)} %param.12) | copy-start | bytes 772
  7.2 56.2 %all-gather.3.cloned.1.call-start = ((), (), s32[]{:S(2)}) async-start(), calls=%async_computation.2 | async-start | bytes 2621440 | tf_op jit(solution)/shard_map/all_gather | solution.py:15
  8.3 21.4 %collective-permute-start = (bf16[64,2048]{1,0:T(8,128)(2,1)S(1)}, bf16[64,2048]{1,0:T(8,128)(2,1)S(1)}, u32[]{:S(2)}, u32[]{:S(2)}) collective-permute-start(bf16[64,2048]{1,0:T(8,128)(2,1)S(1)} %bitcast_convert_fusion), channel_id=1, source_target_pairs={{0,16},{8,24},{16,32},{24,40},{32,48},{40,56},{48,64},{56,72},{64,... | collective-permute-start | bytes 786440 | tf_op jit(solution)/shard_map/ppermute | solution.py:22
  13.2 16.5 %collective-permute-start.1 = (bf16[64,2048]{1,0:T(8,128)(2,1)S(1)}, bf16[64,2048]{1,0:T(8,128)(2,1)S(1)}, u32[]{:S(2)}, u32[]{:S(2)}) collective-permute-start(bf16[64,2048]{1,0:T(8,128)(2,1)S(1)} %bitcast_convert_fusion), channel_id=1, source_target_pairs={{0,8},{8,16},{16,24},{24,32},{32,40},{40,48},{48,56},{56,64},{64,7... | collective-permute-start | bytes 786440 | tf_op jit(solution)/shard_map/ppermute | solution.py:22
  15.7 15.1 %collective-permute-start.2 = (bf16[64,2048]{1,0:T(8,128)(2,1)S(1)}, bf16[64,2048]{1,0:T(8,128)(2,1)S(1)}, u32[]{:S(2)}, u32[]{:S(2)}) collective-permute-start(bf16[64,2048]{1,0:T(8,128)(2,1)S(1)} %bitcast_convert_fusion), channel_id=1, source_target_pairs={{8,0},{16,8},{24,16},{32,24},{40,32},{48,40},{56,48},{64,56},{72,6... | collective-permute-start | bytes 786440 | tf_op jit(solution)/shard_map/ppermute | solution.py:22
  21.2 11.5 %collective-permute-start.3 = (bf16[64,2048]{1,0:T(8,128)(2,1)S(1)}, bf16[64,2048]{1,0:T(8,128)(2,1)S(1)}, u32[]{:S(2)}, u32[]{:S(2)}) collective-permute-start(bf16[64,2048]{1,0:T(8,128)(2,1)S(1)} %bitcast_convert_fusion), channel_id=1, source_target_pairs={{16,0},{24,8},{32,16},{40,24},{48,32},{56,40},{64,48},{72,56},{80,... | collective-permute-start | bytes 786440 | tf_op jit(solution)/shard_map/ppermute | solution.py:22
  50.9 14.3 %copy-start.1 = (f32[1,64,2048]{2,1,0:T(8,128)S(1)}, f32[1,64,2048]{2,1,0:T(8,128)}, u32[]{:S(2)}) copy-start(f32[1,64,2048]{2,1,0:T(8,128)} %param.7) | copy-start | bytes 1572868
  50.9 14.3 %copy-start.3 = (f32[1,64,2048]{2,1,0:T(8,128)S(1)}, f32[1,64,2048]{2,1,0:T(8,128)}, u32[]{:S(2)}) copy-start(f32[1,64,2048]{2,1,0:T(8,128)} %param.8) | copy-start | bytes 1572868
  63.3 12.6 %copy-start.4 = (s32[1,2048]{1,0:T(1,128)S(1)}, s32[1,2048]{1,0:T(1,128)}, u32[]{:S(2)}) copy-start(s32[1,2048]{1,0:T(1,128)} %param.11) | copy-start | bytes 24580
  66.0 9.8 %all-to-all-start = ((f32[2,1,2048]{2,1,0:T(1,128)}), f32[2,1,2048]{2,1,0:T(1,128)S(1)}, u32[]{:S(2)}, u32[]{:S(2)}) async-start(f32[2,1,2048]{2,1,0:T(1,128)} %broadcast_in_dim.67), calls=%async_computation | async-start | bytes 32768 | tf_op jit(solution)/shard_map/all_to_all | solution.py:27
  130.8 6.2 %copy-start.2 = (f32[1,64,2048]{2,1,0:T(8,128)}, f32[1,64,2048]{2,1,0:T(8,128)S(1)}, u32[]{:S(2)}) copy-start(f32[1,64,2048]{2,1,0:T(8,128)S(1)} %fusion.20) | copy-start | bytes 1572868
Sparse Core Ops, SparseCore 0:
  23.3 35.7 all-gather.2
where the time goes:
time: 169 us; the launch traced here: 168 us
  blocking collectives  62 us (37%)
  local copies, waits for them, and re-layouts  27.9 us (17%)
  matrix products  27 us (16%)
  starting transfers between devices  19.3 us (11%)
  between operations  14.3 us (8%)
  other arithmetic  11.1 us (7%)
  waiting for transfers between devices  6.85 us (4%)
    all_gather x1, blocking collectives, rows_first(): result, at, done = (lax.all_gather(both, axis, axis=0, tiled=True), 0, [])  42.7 us
    all_to_all x1, blocking collectives, sent_and_summed(): lax.all_to_all(parts, axis, split_axis=0, concat_axis=0, tiled=True)  19.3 us
    gather x24, local copies, waits for them, and re-layouts  18.1 us
    ppermute x4, starting transfers between devices, passed_along(): return lax.ppermute(block, axis, route)  14.8 us
    dot_general x1, matrix products, per_device(): jnp.einsum('ntw,nrw->tnr', windows, band_tiles, preferred_element_type=jn...  12.4 us
    dot_general x1, matrix products, per_device(): jnp.dot(same_group, trait_total, precision=lax.Precision.HIGHEST)  6.93 us
    dot_general x1, matrix products, per_device(): lax.dot_general(updated.astype(jnp.bfloat16), genotype, (((1,), (1,)), ((...  6.23 us
    all_to_all x1, waiting for transfers between devices, sent_to_all(): return lax.all_to_all(copies, axis, split_axis=0, concat_axis=0, tiled=True)  4.96 us
  transfers between devices with their start and end apart: 6, of which 2 were waited for; matrix products, arithmetic and copies ran while one was open for 23% of the time, Pallas kernels for 0%

commit v1 on v0

--- a/solution.py
+++ b/solution.py
@@ -34,7 +34,13 @@
 def rows_first(arrays, axis, dims):
     turned = [jnp.moveaxis(a, dim, 0) for a, dim in zip(arrays, dims)]
     both = jnp.concatenate([t.reshape(len(t), -1) for t in turned], axis=1)
-    result, at, done = (lax.all_gather(both, axis, axis=0, tiled=True), 0, [])
+    result, at, done = (
+        jnp.concatenate(
+            lax.all_to_all(jnp.stack([both] * lax.axis_size(axis)), axis, 0, 0), axis=0
+        ),
+        0,
+        [],
+    )
     for t, dim in zip(turned, dims):
         piece = result[:, at : at + t[0].size].reshape(-1, *t.shape[1:])
         done.append(jnp.moveaxis(piece, 0, dim))

time: 169 us -> 147 us (0.87)
  blocking collectives: 62 us -> 17.5 us
  starting transfers between devices: 19.3 us -> 31.8 us
  waiting for transfers between devices: 6.85 us -> 15.4 us
    all_gather x1 -> x0, blocking collectives: 42.7 us -> none  [rows_first(): result, at, done = (lax.all_gather(both, axis, axis=0, tiled=True), 0, [])]
    all_to_all x0 -> x1, starting transfers between devices: none -> 12.5 us  [rows_first(): lax.all_to_all(jnp.stack([both] * lax.axis_size(axis)), axis, 0, 0)]
    all_to_all x0 -> x1, waiting for transfers between devices: none -> 8.06 us  [rows_first(): lax.all_to_all(jnp.stack([both] * lax.axis_size(axis)), axis, 0, 0)]
    all_to_all x1, blocking collectives: 19.3 us -> 17.5 us  [sent_and_summed(): lax.all_to_all(parts, axis, split_axis=0, concat_axis=0, tiled=True)]
  transfers between devices with their start and end apart: 6 -> 7, of which waited for: 2 -> 3; matrix products, arithmetic and copies ran while one was open for 23% -> 27% of each run, Pallas kernels for 0% -> 0%
where the time goes in v1:
time: 147 us; the launch traced here: 145 us
  starting transfers between devices  31.8 us (22%)
  local copies, waits for them, and re-layouts  28.4 us (19%)
  matrix products  27 us (18%)
  blocking collectives  17.5 us (12%)
  waiting for transfers between devices  15.4 us (10%)
  between operations  14.3 us (10%)
  other arithmetic  11.1 us (8%)
    gather x24, local copies, waits for them, and re-layouts  18.1 us
    all_to_all x1, blocking collectives, sent_and_summed(): lax.all_to_all(parts, axis, split_axis=0, concat_axis=0, tiled=True)  17.5 us
    ppermute x4, starting transfers between devices, passed_along(): return lax.ppermute(block, axis, route)  14.8 us
    all_to_all x1, starting transfers between devices, rows_first(): lax.all_to_all(jnp.stack([both] * lax.axis_size(axis)), axis, 0, 0)  12.5 us
    dot_general x1, matrix products, per_device(): jnp.einsum('ntw,nrw->tnr', windows, band_tiles, preferred_element_type=jn...  12.4 us
    all_to_all x1, waiting for transfers between devices, rows_first(): lax.all_to_all(jnp.stack([both] * lax.axis_size(axis)), axis, 0, 0)  8.06 us
    dot_general x1, matrix products, per_device(): jnp.dot(same_group, trait_total, precision=lax.Precision.HIGHEST)  6.93 us
    dot_general x1, matrix products, per_device(): lax.dot_general(updated.astype(jnp.bfloat16), genotype, (((1,), (1,)), ((...  6.23 us
  transfers between devices with their start and end apart: 7, of which 3 were waited for; matrix products, arithmetic and copies ran while one was open for 27% of the time, Pallas kernels for 0%

profile of v1, /device:TPU:32, one launch (start us, length us, event | category | flops | bytes accessed | tf_op | source)
XLA Modules:
  0.0 145.5 jit_solution(9786577859912836264)
XLA Ops:
  7.2 1.1 bitcast_convert_fusion
  8.3 4.9 %collective-permute-start = (bf16[64,2048]{1,0:T(8,128)(2,1)S(1)}, bf16[64,2048]{1,0:T(8,128)(2,1)S(1)}, u32[]{:S(2)}, u32[]{:S(2)}) collective-permute-start(bf16[64,2048]{1,0:T(8,128)(2,1)S(1)} %bitcast_convert_fusion), channel_id=1, source_target_pairs={{0,16},{8,24},{16,32},{24,40},{32,48},{40,56},{48,64},{56,72},{64,... | collective-permute-start | bytes 786440 | tf_op jit(solution)/shard_map/ppermute | solution.py:22
  13.2 2.5 %collective-permute-start.1 = (bf16[64,2048]{1,0:T(8,128)(2,1)S(1)}, bf16[64,2048]{1,0:T(8,128)(2,1)S(1)}, u32[]{:S(2)}, u32[]{:S(2)}) collective-permute-start(bf16[64,2048]{1,0:T(8,128)(2,1)S(1)} %bitcast_convert_fusion), channel_id=1, source_target_pairs={{0,8},{8,16},{16,24},{24,32},{32,40},{40,48},{48,56},{56,64},{64,7... | collective-permute-start | bytes 786440 | tf_op jit(solution)/shard_map/ppermute | solution.py:22
  15.7 5.5 %collective-permute-start.2 = (bf16[64,2048]{1,0:T(8,128)(2,1)S(1)}, bf16[64,2048]{1,0:T(8,128)(2,1)S(1)}, u32[]{:S(2)}, u32[]{:S(2)}) collective-permute-start(bf16[64,2048]{1,0:T(8,128)(2,1)S(1)} %bitcast_convert_fusion), channel_id=1, source_target_pairs={{8,0},{16,8},{24,16},{32,24},{40,32},{48,40},{56,48},{64,56},{72,6... | collective-permute-start | bytes 786440 | tf_op jit(solution)/shard_map/ppermute | solution.py:22
  21.2 1.9 %collective-permute-start.3 = (bf16[64,2048]{1,0:T(8,128)(2,1)S(1)}, bf16[64,2048]{1,0:T(8,128)(2,1)S(1)}, u32[]{:S(2)}, u32[]{:S(2)}) collective-permute-start(bf16[64,2048]{1,0:T(8,128)(2,1)S(1)} %bitcast_convert_fusion), channel_id=1, source_target_pairs={{16,0},{24,8},{32,16},{40,24},{48,32},{56,40},{64,48},{72,56},{80,... | collective-permute-start | bytes 786440 | tf_op jit(solution)/shard_map/ppermute | solution.py:22
  23.2 0.7 convert_element_type.22
  23.9 2.5 %fusion.2 = f32[2048]{0:T(1024)S(1)} fusion(s32[2048]{0:T(1024)} %bitcast.94), kind=kLoop, calls=%fused_computation.5 | loop fusion | flops 12580864 | bytes 16384 | tf_op jit(solution)/shard_map/reduce_sum | solution.py:99
  26.4 1.4 fusion.10
  27.8 0.7 compare_select_fusion.4
  29.2 1.1 constant_dynamic-update-slice_fusion.2
  30.3 2.5 %collective-permute-done.3 = bf16[64,2048]{1,0:T(8,128)(2,1)S(1)} collective-permute-done((bf16[64,2048]{1,0:T(8,128)(2,1)S(1)}, bf16[64,2048]{1,0:T(8,128)(2,1)S(1)}, u32[]{:S(2)}, u32[]{:S(2)}) %collective-permute-start.3) | collective-permute-done | bytes 262176 | tf_op jit(solution)/shard_map/ppermute | solution.py:22
  32.8 18.2 %while.1 = (s32[]{:T(128)}, bf16[64,10240]{1,0:T(8,128)(2,1)S(1)}, s32[8,2]{0,1:T(2,128)S(1)}, bf16[8,64,4096]{2,1,0:T(8,128)(2,1)}, s32[]{:T(128)}) while((s32[]{:T(128)}, bf16[64,10240]{1,0:T(8,128)(2,1)S(1)}, s32[8,2]{0,1:T(2,128)S(1)}, bf16[8,64,4096]{2,1,0:T(8,128)(2,1)}, s32[]{:T(128)}) %tuple.29), condition=%wide.while_cond, body=%wide.while_body.sunk | while | flops 2 | bytes 1049689 | solution.py:88
  33.4 1.6 %bitcast_dynamic-update-slice_fusion.2 = bf16[8,64,4096]{2,1,0:T(8,128)(2,1)} fusion(bf16[8,64,4096]{2,1,0:T(8,128)(2,1)} %get-tuple-element.65, s32[]{:T(128)} %get-tuple-element.62, bf16[64,10240]{1,0:T(8,128)(2,1)S(1)} %get-tuple-element.68, s32[]{:T(128)} %bitcast.82), kind=kLoop, calls=%fused_computation.clone.1 | loop fusion | bytes 1049600 | tf_op jit(solution)/shard_map/vmap()/gather
  35.7 1.7 %bitcast_dynamic-update-slice_fusion.2 = bf16[8,64,4096]{2,1,0:T(8,128)(2,1)} fusion(bf16[8,64,4096]{2,1,0:T(8,128)(2,1)} %get-tuple-element.65, s32[]{:T(128)} %get-tuple-element.62, bf16[64,10240]{1,0:T(8,128)(2,1)S(1)} %get-tuple-element.68, s32[]{:T(128)} %bitcast.82), kind=kLoop, calls=%fused_computation.clone.1 | loop fusion | bytes 1049600 | tf_op jit(solution)/shard_map/vmap()/gather
  37.9 1.7 %bitcast_dynamic-update-slice_fusion.2 = bf16[8,64,4096]{2,1,0:T(8,128)(2,1)} fusion(bf16[8,64,4096]{2,1,0:T(8,128)(2,1)} %get-tuple-element.65, s32[]{:T(128)} %get-tuple-element.62, bf16[64,10240]{1,0:T(8,128)(2,1)S(1)} %get-tuple-element.68, s32[]{:T(128)} %bitcast.82), kind=kLoop, calls=%fused_computation.clone.1 | loop fusion | bytes 1049600 | tf_op jit(solution)/shard_map/vmap()/gather
  40.2 1.7 %bitcast_dynamic-update-slice_fusion.2 = bf16[8,64,4096]{2,1,0:T(8,128)(2,1)} fusion(bf16[8,64,4096]{2,1,0:T(8,128)(2,1)} %get-tuple-element.65, s32[]{:T(128)} %get-tuple-element.62, bf16[64,10240]{1,0:T(8,128)(2,1)S(1)} %get-tuple-element.68, s32[]{:T(128)} %bitcast.82), kind=kLoop, calls=%fused_computation.clone.1 | loop fusion | bytes 1049600 | tf_op jit(solution)/shard_map/vmap()/gather
  42.5 1.6 %bitcast_dynamic-update-slice_fusion.2 = bf16[8,64,4096]{2,1,0:T(8,128)(2,1)} fusion(bf16[8,64,4096]{2,1,0:T(8,128)(2,1)} %get-tuple-element.65, s32[]{:T(128)} %get-tuple-element.62, bf16[64,10240]{1,0:T(8,128)(2,1)S(1)} %get-tuple-element.68, s32[]{:T(128)} %bitcast.82), kind=kLoop, calls=%fused_computation.clone.1 | loop fusion | bytes 1049600 | tf_op jit(solution)/shard_map/vmap()/gather
  44.7 1.7 %bitcast_dynamic-update-slice_fusion.2 = bf16[8,64,4096]{2,1,0:T(8,128)(2,1)} fusion(bf16[8,64,4096]{2,1,0:T(8,128)(2,1)} %get-tuple-element.65, s32[]{:T(128)} %get-tuple-element.62, bf16[64,10240]{1,0:T(8,128)(2,1)S(1)} %get-tuple-element.68, s32[]{:T(128)} %bitcast.82), kind=kLoop, calls=%fused_computation.clone.1 | loop fusion | bytes 1049600 | tf_op jit(solution)/shard_map/vmap()/gather
  47.0 1.6 %bitcast_dynamic-update-slice_fusion.2 = bf16[8,64,4096]{2,1,0:T(8,128)(2,1)} fusion(bf16[8,64,4096]{2,1,0:T(8,128)(2,1)} %get-tuple-element.65, s32[]{:T(128)} %get-tuple-element.62, bf16[64,10240]{1,0:T(8,128)(2,1)S(1)} %get-tuple-element.68, s32[]{:T(128)} %bitcast.82), kind=kLoop, calls=%fused_computation.clone.1 | loop fusion | bytes 1049600 | tf_op jit(solution)/shard_map/vmap()/gather
  49.3 1.7 %bitcast_dynamic-update-slice_fusion.2 = bf16[8,64,4096]{2,1,0:T(8,128)(2,1)} fusion(bf16[8,64,4096]{2,1,0:T(8,128)(2,1)} %get-tuple-element.65, s32[]{:T(128)} %get-tuple-element.62, bf16[64,10240]{1,0:T(8,128)(2,1)S(1)} %get-tuple-element.68, s32[]{:T(128)} %bitcast.82), kind=kLoop, calls=%fused_computation.clone.1 | loop fusion | bytes 1049600 | tf_op jit(solution)/shard_map/vmap()/gather
  50.9 12.4 %fusion.33 = f32[8,64,256]{2,1,0:T(8,128)S(1)} fusion(bf16[8,64,4096]{2,1,0:T(8,128)(2,1)} %get-tuple-element.9, bf16[8,256,4096]{2,1,0:T(8,128)(2,1)} %bitcast.83), kind=kOutput, calls=%fused_computation.59 | convolution fusion | flops 1073741824 | bytes 21495808 | tf_op jit(solution)/shard_map/ntw,nrw->tnr/dot_general | solution.py:91
  63.4 1.8 %reduce_sum.63 = f32[64,2048]{1,0:T(8,128)S(1)} reduce(f32[4,64,2048]{2,1,0:T(8,128)} %all-gather.2.cloned.1.call-done, f32[]{:T(128)} %constant.8.clone.1), dimensions={0}, to_apply=%region_0.0 | reduce | flops 393216 | bytes 2621444 | tf_op jit(solution)/shard_map/reduce_sum | solution.py:16
  66.0 4.4 %all-to-all-start = ((f32[2,1,2048]{2,1,0:T(1,128)}), f32[2,1,2048]{2,1,0:T(1,128)S(1)}, u32[]{:S(2)}, u32[]{:S(2)}) async-start(f32[2,1,2048]{2,1,0:T(1,128)} %broadcast_in_dim.67), calls=%async_computation | async-start | bytes 32768 | tf_op jit(solution)/shard_map/all_to_all | solution.py:27
  71.1 4.8 %all-to-all-done = f32[2,1,2048]{2,1,0:T(1,128)S(1)} async-done(((f32[2,1,2048]{2,1,0:T(1,128)}), f32[2,1,2048]{2,1,0:T(1,128)S(1)}, u32[]{:S(2)}, u32[]{:S(2)}) %all-to-all-start) | async-done | bytes 16416 | tf_op jit(solution)/shard_map/all_to_all | solution.py:27
  75.9 6.9 %fusion = f32[1,2048]{1,0:T(1,128)S(1)} fusion(f32[2048,1]{0,1:T(1,128)S(1)} %bitcast.92, s32[2048]{0:T(1024)S(1)} %bitcast.96), kind=kOutput, calls=%fused_computation.2 | convolution fusion | flops 54525952 | bytes 24576 | tf_op jit(solution)/shard_map/dot_general | solution.py:98
  83.4 3.8 %concatenate.13 = f32[1,6]{1,0:T(1,128)S(1)} concatenate(f32[1,1]{1,0:T(1,128)} %bitcast.10, f32[1,1]{1,0:T(1,128)} %bitcast.11, f32[1,1]{1,0:T(1,128)} %bitcast.15, f32[1,1]{1,0:T(1,128)} %bitcast.16, f32[1,1]{1,0:T(1,128)} %bitcast.17, f32[1,1]{1,0:T(1,128)} %bitcast.18), dimensions={1} | concatenate | bytes 48 | tf_op jit(solution)/shard_map/concatenate | solution.py:36
  87.9 12.5 %all-to-all-start.1 = ((f32[32,1,6]{2,1,0:T(1,128)}), f32[32,1,6]{2,1,0:T(1,128)S(1)}, u32[]{:S(2)}, u32[]{:S(2)}) async-start(f32[32,1,6]{2,1,0:T(1,128)} %stack.2), calls=%async_computation.1 | async-start | bytes 32768 | tf_op jit(solution)/shard_map/all_to_all | solution.py:39
  100.9 8.1 %all-to-all-done.1 = f32[32,1,6]{2,1,0:T(1,128)S(1)} async-done(((f32[32,1,6]{2,1,0:T(1,128)}), f32[32,1,6]{2,1,0:T(1,128)S(1)}, u32[]{:S(2)}, u32[]{:S(2)}) %all-to-all-start.1) | async-done | bytes 800 | tf_op jit(solution)/shard_map/all_to_all | solution.py:39
  109.6 6.2 %fusion.7 = f32[64,2048]{1,0:T(8,128)S(1)} fusion(bf16[1,2048,2048]{2,1,0:T(8,128)(2,1)} %param.13, f32[1,64,2048]{2,1,0:T(8,128)S(1)} %fusion.20), kind=kOutput, calls=%fused_computation.10 | convolution fusion | flops 537133056 | bytes 9437184 | tf_op jit(solution)/shard_map/dot_general | solution.py:137
  117.5 17.5 %all_to_all.16 = f32[32,1,4096]{2,1,0:T(1,128)S(1)} all-to-all(f32[32,1,4096]{2,1,0:T(1,128)S(1)} %reshape.140), channel_id=1, replica_groups=mesh['genome'=32,'anc'=4,'trait'=2] {'genome'}, dimensions={0} | all-to-all | bytes 1048576 | tf_op jit(solution)/shard_map/all_to_all | solution.py:59
  135.6 1.9 %reduce.13 = f32[32,4096]{1,0:T(8,128)S(1)} reduce(f32[32,1,4096]{2,1,0:T(1,128)S(1)} %all_to_all.16, f32[]{:T(128)} %broadcast.113), dimensions={1}, to_apply=%all_to_all.12.reduce_sub_computation | reduce | bytes 1048580 | tf_op jit(solution)/shard_map/all_to_all | solution.py:59
  137.9 0.7 reduce_sum.69
  (58 shorter events, 12.0 us)
Async XLA Ops:
  7.2 19.3 %copy-start = (f32[1,64]{1,0:T(1,128)S(1)}, f32[1,64]{1,0:T(1,128)}, u32[]{:S(2)}) copy-start(f32[1,64]{1,0:T(1,128)} %param.12) | copy-start | bytes 772
  7.2 56.2 %all-gather.2.cloned.1.call-start = ((), (), s32[]{:S(2)}) async-start(), calls=%async_computation.3 | async-start | bytes 2621440 | tf_op jit(solution)/shard_map/all_gather | solution.py:15
  8.3 20.8 %collective-permute-start = (bf16[64,2048]{1,0:T(8,128)(2,1)S(1)}, bf16[64,2048]{1,0:T(8,128)(2,1)S(1)}, u32[]{:S(2)}, u32[]{:S(2)}) collective-permute-start(bf16[64,2048]{1,0:T(8,128)(2,1)S(1)} %bitcast_convert_fusion), channel_id=1, source_target_pairs={{0,16},{8,24},{16,32},{24,40},{32,48},{40,56},{48,64},{56,72},{64,... | collective-permute-start | bytes 786440 | tf_op jit(solution)/shard_map/ppermute | solution.py:22
  13.2 15.9 %collective-permute-start.1 = (bf16[64,2048]{1,0:T(8,128)(2,1)S(1)}, bf16[64,2048]{1,0:T(8,128)(2,1)S(1)}, u32[]{:S(2)}, u32[]{:S(2)}) collective-permute-start(bf16[64,2048]{1,0:T(8,128)(2,1)S(1)} %bitcast_convert_fusion), channel_id=1, source_target_pairs={{0,8},{8,16},{16,24},{24,32},{32,40},{40,48},{48,56},{56,64},{64,7... | collective-permute-start | bytes 786440 | tf_op jit(solution)/shard_map/ppermute | solution.py:22
  15.7 14.5 %collective-permute-start.2 = (bf16[64,2048]{1,0:T(8,128)(2,1)S(1)}, bf16[64,2048]{1,0:T(8,128)(2,1)S(1)}, u32[]{:S(2)}, u32[]{:S(2)}) collective-permute-start(bf16[64,2048]{1,0:T(8,128)(2,1)S(1)} %bitcast_convert_fusion), channel_id=1, source_target_pairs={{8,0},{16,8},{24,16},{32,24},{40,32},{48,40},{56,48},{64,56},{72,6... | collective-permute-start | bytes 786440 | tf_op jit(solution)/shard_map/ppermute | solution.py:22
  21.2 11.5 %collective-permute-start.3 = (bf16[64,2048]{1,0:T(8,128)(2,1)S(1)}, bf16[64,2048]{1,0:T(8,128)(2,1)S(1)}, u32[]{:S(2)}, u32[]{:S(2)}) collective-permute-start(bf16[64,2048]{1,0:T(8,128)(2,1)S(1)} %bitcast_convert_fusion), channel_id=1, source_target_pairs={{16,0},{24,8},{32,16},{40,24},{48,32},{56,40},{64,48},{72,56},{80,... | collective-permute-start | bytes 786440 | tf_op jit(solution)/shard_map/ppermute | solution.py:22
  50.9 14.3 %copy-start.1 = (f32[1,64,2048]{2,1,0:T(8,128)S(1)}, f32[1,64,2048]{2,1,0:T(8,128)}, u32[]{:S(2)}) copy-start(f32[1,64,2048]{2,1,0:T(8,128)} %param.7) | copy-start | bytes 1572868
  50.9 14.3 %copy-start.3 = (f32[1,64,2048]{2,1,0:T(8,128)S(1)}, f32[1,64,2048]{2,1,0:T(8,128)}, u32[]{:S(2)}) copy-start(f32[1,64,2048]{2,1,0:T(8,128)} %param.8) | copy-start | bytes 1572868
  63.3 12.6 %copy-start.4 = (s32[1,2048]{1,0:T(1,128)S(1)}, s32[1,2048]{1,0:T(1,128)}, u32[]{:S(2)}) copy-start(s32[1,2048]{1,0:T(1,128)} %param.11) | copy-start | bytes 24580
  66.0 9.8 %all-to-all-start = ((f32[2,1,2048]{2,1,0:T(1,128)}), f32[2,1,2048]{2,1,0:T(1,128)S(1)}, u32[]{:S(2)}, u32[]{:S(2)}) async-start(f32[2,1,2048]{2,1,0:T(1,128)} %broadcast_in_dim.67), calls=%async_computation | async-start | bytes 32768 | tf_op jit(solution)/shard_map/all_to_all | solution.py:27
  87.9 21.0 %all-to-all-start.1 = ((f32[32,1,6]{2,1,0:T(1,128)}), f32[32,1,6]{2,1,0:T(1,128)S(1)}, u32[]{:S(2)}, u32[]{:S(2)}) async-start(f32[32,1,6]{2,1,0:T(1,128)} %stack.2), calls=%async_computation.1 | async-start | bytes 32768 | tf_op jit(solution)/shard_map/all_to_all | solution.py:39
  109.6 6.2 %copy-start.2 = (f32[1,64,2048]{2,1,0:T(8,128)}, f32[1,64,2048]{2,1,0:T(8,128)S(1)}, u32[]{:S(2)}) copy-start(f32[1,64,2048]{2,1,0:T(8,128)S(1)} %fusion.20) | copy-start | bytes 1572868
Sparse Core Ops, SparseCore 0:
  23.3 35.7 all-gather.1
